TPU v7x, 128 devices: a whole 4x4x4 slice. The times are simulated.
128 devices in a mesh: dp: 16 (over y, z), mp: 8 (over x, core).
Axes of the slice: x: 4, y: 4, z: 4, core: 2. Of those that a mesh axis runs over, the one named last changes fastest.
Arguments:
- hidden_in: bfloat16 [4096, 2304], P('dp'), may hold values from -6 to 6
- attn_gain: float32 [2304], replicated, may hold values from 0.25 to 1.75
- w_query: bfloat16 [2304, 2048], P(None, 'mp'), may hold values from -0.25 to 0.25
- w_key: bfloat16 [2304, 2048], P(None, 'mp'), may hold values from -0.125 to 0.125
- w_value: bfloat16 [2304, 2048], P(None, 'mp'), may hold values from -0.125 to 0.125
- w_out: bfloat16 [2048, 2304], P('mp'), may hold values from -0.5 to 0.5
- root_cache: bfloat16 [2, 4096, 2048], P(None, 'dp', 'mp'), may hold values from -400 to 400
- mid_cache: bfloat16 [2, 16, 1024, 2048], P(None, 'dp', None, 'mp'), may hold values from -400 to 400
- leaf_cache: bfloat16 [2, 32, 1024, 2048], P(None, 'dp', None, 'mp'), may hold values from -400 to 400
- mid_len: int32 [16], P('dp'), may hold values from 1 to 1024, 8192 in all
- leaf_len: int32 [32], P('dp'), may hold values from 1 to 1024, 16384 in all
- leaf_of: int32 [128], P('dp'), may hold values from 0 to 31, as said below
- parents: int32 [32], replicated, may hold values from 0 to 15, as said below
- suffix_len: int32 [128], P('dp'), may hold values from 1 to 32, 3072 in all
- ffn_gain: float32 [2304], replicated, may hold values from 0.25 to 1.75
- w_router: float32 [2304, 8], replicated, may hold values from -0.5 to 0.5
- routes: int32 [4096, 2], P('dp'), may hold values from 0 to 7, all different within a row; in each aligned block of 256 rows (0 to 255, 256 to 511, ...) at most 96 rows name the same one
- w_gate: bfloat16 [8, 2304, 5760], P('mp', None, 'dp'), may hold values from -0.125 to 0.125
- w_up: bfloat16 [8, 2304, 5760], P('mp', None, 'dp'), may hold values from -0.125 to 0.125
- w_down: bfloat16 [8, 5760, 2304], P('mp', 'dp'), may hold values from -0.078125 to 0.078125
Outputs:
- layer_out: bfloat16 [4096, 2304], P(('dp', 'mp'))
Inputs may be any that keep to these rules, and one draw needn't show every extreme that they name: `leaf_of`: leaf n belongs to index n // 2 of dp, mid-level node n to index n. The 8 sequences of one index of dp have different mid-level nodes and leaves of one parity, so that no two of them share a mid-level node or a leaf's owner. `parents`: every mid-level node is the parent of exactly one even and one odd leaf. `routes`: in the rows of one index of dp no expert is named by more than 96 rows; some indices of dp reach 96.
All inputs are finite; a program needn't handle non-finite values. No bound on the sum of `mid_len` or of `leaf_len` or of `suffix_len` on one device may be relied on, other than what follows from the above.
Results may differ from a plain program's by a relative error of at most 0.015.
The roundings to bfloat16 on the way count: a program that leaves them out, or rounds other values in their place, can miss the bound.
Values may be sent and summed in bfloat16 or wider, within the bound.
A program may use at most 128 MiB of HBM per device.

v0:
```python
import math
import jax
import jax.numpy as jnp
from jax import lax
from jax.sharding import PartitionSpec as P

HD = 64
TOP = 2
EPS = 1e-05
NEGATIVE = -1e30


def rms_scale(rows, gain):
    rows_wide = rows.astype(jnp.float32)
    mean_square = jnp.mean(rows_wide * rows_wide, axis=-1, keepdims=True)
    return rows_wide * lax.rsqrt(mean_square + EPS) * gain


def level_partial(queries, node_keys, node_values, limits, heads_here, batched):
    senders, row_count, width = queries.shape
    head_dim = width // heads_here
    scale = 1.0 / math.sqrt(head_dim)
    query_heads = queries.reshape(senders, row_count, heads_here, head_dim)
    if batched:
        key_heads = node_keys.reshape(senders, -1, heads_here, head_dim)
        value_heads = node_values.reshape(senders, -1, heads_here, head_dim)
        scores = jnp.einsum(
            "sqhd,skhd->sqhk", query_heads, key_heads, preferred_element_type=jnp.float32
        )
    else:
        key_heads = node_keys.reshape(-1, heads_here, head_dim)
        value_heads = node_values.reshape(-1, heads_here, head_dim)
        scores = jnp.einsum(
            "sqhd,khd->sqhk", query_heads, key_heads, preferred_element_type=jnp.float32
        )
    scores = scores * scale
    slots = jnp.arange(scores.shape[-1], dtype=jnp.int32)
    allowed = slots[None, :] < limits[:, None]
    scores = jnp.where(allowed[:, None, None, :], scores, NEGATIVE)
    peak = jnp.max(scores, axis=-1)
    weights = jnp.exp(scores - peak[..., None])
    total = jnp.sum(weights, axis=-1)
    probs = weights.astype(jnp.bfloat16)
    if batched:
        summed = jnp.einsum(
            "sqhk,skhd->sqhd", probs, value_heads, preferred_element_type=jnp.float32
        )
    else:
        summed = jnp.einsum(
            "sqhk,khd->sqhd", probs, value_heads, preferred_element_type=jnp.float32
        )
    result = (summed / total[..., None]).reshape(senders, row_count, width)
    return (result, peak + jnp.log(total))


def on_device(
    hidden_in,
    attn_gain,
    w_query,
    w_key,
    w_value,
    w_out,
    root_cache,
    mid_cache,
    leaf_cache,
    mid_len,
    leaf_len,
    leaf_of,
    parents,
    suffix_len,
    ffn_gain,
    w_router,
    routes,
    w_gate,
    w_up,
    w_down,
):
    tok_rows, width = hidden_in.shape
    seq_rows = suffix_len.shape[0]
    suffix = tok_rows // seq_rows
    head_dim = HD
    local_width = w_query.shape[1]
    heads_here = local_width // head_dim
    scale = 1.0 / math.sqrt(head_dim)
    owners = lax.axis_size("dp")
    normed = rms_scale(hidden_in, attn_gain).astype(jnp.bfloat16)
    query = jnp.dot(normed, w_query, preferred_element_type=jnp.float32).astype(jnp.bfloat16)
    key = jnp.dot(normed, w_key, preferred_element_type=jnp.float32).astype(jnp.bfloat16)
    value = jnp.dot(normed, w_value, preferred_element_type=jnp.float32).astype(jnp.bfloat16)
    query_heads = query.reshape(tok_rows, heads_here, head_dim)
    piece = lax.all_gather(root_cache, "dp", axis=1, tiled=True)
    running_peak = jnp.full((tok_rows, heads_here), NEGATIVE, jnp.float32)
    piece_keys = piece[0].reshape(-1, heads_here, head_dim)
    piece_values = piece[1].reshape(-1, heads_here, head_dim)
    scores = (
        jnp.einsum("qhd,khd->qhk", query_heads, piece_keys, preferred_element_type=jnp.float32)
        * scale
    )
    new_peak = jnp.maximum(running_peak, jnp.max(scores, axis=-1))
    weights = jnp.exp(scores - new_peak[..., None])
    new_total = jnp.sum(weights, axis=-1)
    added = jnp.einsum(
        "qhk,khd->qhd",
        weights.astype(jnp.bfloat16),
        piece_values,
        preferred_element_type=jnp.float32,
    )
    root_out = added / new_total[..., None]
    root_lse = new_peak + jnp.log(new_total)
    query_seq = query.reshape(seq_rows, suffix, heads_here, head_dim)
    key_seq = key.reshape(seq_rows, suffix, heads_here, head_dim)
    value_seq = value.reshape(seq_rows, suffix, heads_here, head_dim)
    slots = jnp.arange(suffix, dtype=jnp.int32)
    self_ok = (slots[None, None, :] <= slots[None, :, None]) & (
        slots[None, None, :] < suffix_len[:, None, None]
    )
    self_scores = (
        jnp.einsum("sqhd,skhd->sqhk", query_seq, key_seq, preferred_element_type=jnp.float32)
        * scale
    )
    self_scores = jnp.where(self_ok[:, :, None, :], self_scores, NEGATIVE)
    self_peak = jnp.max(self_scores, axis=-1)
    self_weights = jnp.exp(self_scores - self_peak[..., None])
    self_total = jnp.sum(self_weights, axis=-1)
    self_sum = jnp.einsum(
        "sqhk,skhd->sqhd",
        self_weights.astype(jnp.bfloat16),
        value_seq,
        preferred_element_type=jnp.float32,
    )
    self_out = (self_sum / self_total[..., None]).reshape(tok_rows, heads_here, head_dim)
    self_lse = (self_peak + jnp.log(self_total)).reshape(tok_rows, heads_here)
    mid_of = parents[leaf_of]
    leaf_owner = leaf_of // 2
    leaf_side = (leaf_of % 2).astype(jnp.float32)
    targets = jnp.arange(owners, dtype=jnp.int32)
    pick_mid = (mid_of[None, :] == targets[:, None]).astype(jnp.bfloat16)
    pick_leaf = (leaf_owner[None, :] == targets[:, None]).astype(jnp.bfloat16)
    flat_query = query.reshape(seq_rows, suffix * local_width)
    sent_mid = jnp.dot(pick_mid, flat_query, preferred_element_type=jnp.float32).astype(
        jnp.bfloat16
    )
    sent_leaf = jnp.dot(pick_leaf, flat_query, preferred_element_type=jnp.float32).astype(
        jnp.bfloat16
    )
    sent = jnp.stack([sent_mid, sent_leaf], axis=1).reshape(owners, 2, suffix, local_width)
    side_of_target = jnp.dot(
        pick_leaf.astype(jnp.float32), leaf_side, precision=lax.Precision.HIGHEST
    )
    sides = jnp.stack([jnp.zeros_like(side_of_target), side_of_target], axis=1)
    sides = jnp.broadcast_to(sides[:, :, None], (owners, 2, suffix)).astype(jnp.bfloat16)
    sent_queries = lax.all_to_all(sent, "dp", split_axis=0, concat_axis=0, tiled=True)
    sent_sides = lax.all_to_all(sides, "dp", split_axis=0, concat_axis=0, tiled=True)
    senders = sent_queries.shape[0]
    second = sent_sides[:, 1, 0] > 0.5
    mid_limit = jnp.broadcast_to(mid_len[0], (senders,))
    mid_result, mid_logsum = level_partial(
        sent_queries[:, 0], mid_cache[0, 0], mid_cache[1, 0], mid_limit, heads_here, False
    )
    leaf_keys = jnp.where(second[:, None, None], leaf_cache[0, 1][None], leaf_cache[0, 0][None])
    leaf_values = jnp.where(second[:, None, None], leaf_cache[1, 1][None], leaf_cache[1, 0][None])
    leaf_limit = jnp.where(second, leaf_len[1], leaf_len[0])
    leaf_result, leaf_logsum = level_partial(
        sent_queries[:, 1], leaf_keys, leaf_values, leaf_limit, heads_here, True
    )
    owner_out = jnp.stack([mid_result, leaf_result], axis=1)
    owner_lse = jnp.stack([mid_logsum, leaf_logsum], axis=1)
    back_out, back_lse = (
        lax.all_to_all(owner_out, "dp", split_axis=0, concat_axis=0, tiled=True),
        lax.all_to_all(owner_lse, "dp", split_axis=0, concat_axis=0, tiled=True),
    )
    mid_out = back_out[mid_of, 0].reshape(tok_rows, heads_here, head_dim)
    mid_lse = back_lse[mid_of, 0].reshape(tok_rows, heads_here)
    leaf_out = back_out[leaf_owner, 1].reshape(tok_rows, heads_here, head_dim)
    leaf_lse = back_lse[leaf_owner, 1].reshape(tok_rows, heads_here)
    stacked_lse = jnp.stack([root_lse, mid_lse, leaf_lse, self_lse])
    stacked_out = jnp.stack([root_out, mid_out, leaf_out, self_out])
    overall = jnp.max(stacked_lse, axis=0)
    shares = jnp.exp(stacked_lse - overall)
    combined = jnp.sum(shares[..., None] * stacked_out, axis=0) / jnp.sum(shares, axis=0)[..., None]
    attended = combined.reshape(tok_rows, local_width).astype(jnp.bfloat16)
    projected = jnp.dot(attended, w_out, preferred_element_type=jnp.float32)
    rows_here = tok_rows // lax.axis_size("mp")
    first = lax.axis_index("mp") * rows_here
    attn_all = lax.psum(projected, "mp")
    resid_all = hidden_in.astype(jnp.float32) + attn_all
    ffn_in = rms_scale(resid_all, ffn_gain).astype(jnp.bfloat16)
    resid = lax.dynamic_slice_in_dim(resid_all, first, rows_here, 0)
    logits = jnp.dot(ffn_in.astype(jnp.float32), w_router, precision=lax.Precision.HIGHEST)
    chosen = jnp.take_along_axis(logits, routes, axis=1)
    squashed = jax.nn.sigmoid(chosen)
    gates = squashed / jnp.sum(squashed, axis=1, keepdims=True)
    expert = lax.axis_index("mp")
    hit_each = routes == expert
    hit = jnp.any(hit_each, axis=1)
    gate_here = jnp.sum(jnp.where(hit_each, gates, 0.0), axis=1)
    order = jnp.cumsum(hit.astype(jnp.int32)) - 1
    capacity = 3 * TOP * tok_rows // (2 * lax.axis_size("mp"))
    slot_ids = jnp.arange(capacity, dtype=jnp.int32)
    pick_slot = (order[None, :] == slot_ids[:, None]) & hit[None, :]
    dispatch = jnp.dot(
        pick_slot.astype(jnp.bfloat16), ffn_in, preferred_element_type=jnp.float32
    ).astype(jnp.bfloat16)
    slot_gate = jnp.dot(pick_slot.astype(jnp.float32), gate_here, precision=lax.Precision.HIGHEST)
    gate_weight = w_gate[0]
    up_weight = w_up[0]
    down_weight = w_down[0]
    piece = lax.all_gather(dispatch, "dp", axis=0, tiled=True)
    gate_part = jnp.dot(piece, gate_weight, preferred_element_type=jnp.float32)
    up_part = jnp.dot(piece, up_weight, preferred_element_type=jnp.float32)
    partial_out = jnp.dot(
        (jax.nn.silu(gate_part) * up_part).astype(jnp.bfloat16),
        down_weight,
        preferred_element_type=jnp.float32,
    )
    expert_out = lax.psum_scatter(partial_out, "dp", scatter_dimension=0, tiled=True)
    weighted = expert_out * slot_gate[:, None]
    spread = jnp.dot(pick_slot.astype(jnp.float32).T, weighted, precision=lax.Precision.HIGHEST)
    mixed = lax.psum_scatter(spread, "mp", scatter_dimension=0, tiled=True)
    row_ids = first + jnp.arange(rows_here, dtype=jnp.int32)
    valid = row_ids % suffix < suffix_len[row_ids // suffix]
    return jnp.where(valid[:, None], resid + mixed, 0.0).astype(jnp.bfloat16)


def solution(mesh):
    return jax.shard_map(
        on_device,
        mesh=mesh,
        in_specs=(
            P("dp", None),
            P(),
            P(None, "mp"),
            P(None, "mp"),
            P(None, "mp"),
            P("mp", None),
            P(None, "dp", "mp"),
            P(None, "dp", None, "mp"),
            P(None, "dp", None, "mp"),
            P("dp"),
            P("dp"),
            P("dp"),
            P(),
            P("dp"),
            P(),
            P(),
            P("dp", None),
            P("mp", None, "dp"),
            P("mp", None, "dp"),
            P("mp", "dp", None),
        ),
        out_specs=P(("dp", "mp"), None),
        check_vma=False,
    )
```

profile of v0, /device:TPU:0, one launch (start us, length us, event | category | flops | bytes accessed | tf_op | source)
XLA Modules:
  0.0 482.1 jit_solution(8950069300431746591)
XLA Ops:
  9.6 8.1 %all-to-all-start.1 = ((bf16[16,2,32]{2,1,0:T(2,128)(2,1)}), bf16[16,2,32]{2,1,0:T(2,128)(2,1)S(1)}, u32[]{:S(2)}, u32[]{:S(2)}) async-start(bf16[16,2,32]{2,1,0:T(2,128)(2,1)} %broadcast_in_dim.168), calls=%async_computation.1 | async-start | bytes 16384 | tf_op jit(solution)/shard_map/all_to_all | solution.py:153
  17.7 1.6 fusion.30
  19.4 2.5 convolution_convert_fusion.5
  23.0 1.8 convolution_convert_fusion.4
  27.9 1.3 fusion.138
  30.8 1.0 fusion.135
  31.8 1.4 fusion.134
  34.5 7.6 %all-to-all-start = ((bf16[16,2,32,256]{3,2,1,0:T(8,128)(2,1)}), bf16[16,2,32,256]{3,2,1,0:T(8,128)(2,1)}, u32[]{:S(2)}, u32[]{:S(2)}) async-start(bf16[16,2,32,256]{3,2,1,0:T(8,128)(2,1)} %pad_maximum_fusion.1), calls=%async_computation | async-start | bytes 1048576 | tf_op jit(solution)/shard_map/all_to_all | solution.py:152
  42.1 1.2 copy.251
  43.3 2.1 copy.270
  45.4 2.0 copy.290
  47.4 2.0 copy.289
  49.5 2.0 copy.288
  51.5 2.0 copy.291
  54.4 1.6 fusion.97
  56.6 1.9 fusion.136
  58.5 2.0 reshape_squeeze.19
  60.5 2.0 reshape_squeeze.21
  62.5 4.5 bitcast_reduce_fusion.1
  67.1 2.2 fusion.16
  69.3 2.7 fusion.64
  72.0 1.7 copy.274
  73.7 2.6 stack_reshape.25
  76.3 2.4 bitcast_reduce_fusion.2
  78.8 2.6 fusion.14
  82.7 1.5 reshape.482
  84.2 4.5 fusion.69
  88.7 1.7 copy.271
  90.4 2.7 stack_reshape.24
  93.0 7.1 %all-to-all-start.2 = ((f32[16,1,256]{2,1,0:T(1,128)}), f32[16,1,256]{2,1,0:T(1,128)S(1)}, u32[]{:S(2)}, u32[]{:S(2)}) async-start(f32[16,1,256]{2,1,0:T(1,128)} %reshape.482), calls=%async_computation.2 | async-start | bytes 32768 | tf_op jit(solution)/shard_map/all_to_all | solution.py:170
  100.1 2.2 pad_maximum_fusion
  102.3 5.3 %all-to-all-done.2 = f32[16,1,256]{2,1,0:T(1,128)S(1)} async-done(((f32[16,1,256]{2,1,0:T(1,128)}), f32[16,1,256]{2,1,0:T(1,128)S(1)}, u32[]{:S(2)}, u32[]{:S(2)}) %all-to-all-start.2) | async-done | bytes 16416 | tf_op jit(solution)/shard_map/all_to_all | solution.py:170
  107.7 4.3 all-to-all-start.3
  113.5 2.5 convolution_convert_fusion.3
  116.0 1.8 reshape.409
  117.8 1.3 fusion.48
  120.5 1.4 reduce.10
  123.5 3.6 all-to-all-done.3
  127.1 2.5 gather_fusion.5
  129.6 1.2 stack_reshape.27
  131.7 2.5 gather_fusion.4
  134.2 1.2 stack_reshape.26
  135.4 0.9 copy.280
  136.3 4.5 fusion.133
  140.7 4.3 copy.247
  145.0 4.1 copy.269
  149.1 9.7 %bitcast_reduce_fusion = (f32[256,4]{0,1:T(4,128)S(1)}, f32[4,256,4096]{2,1,0:T(8,128)}) fusion(bf16[256,4,64]{0,2,1:T(8,128)(2,1)S(1)} %bitcast.204, bf16[4096,4,64]{0,2,1:T(8,128)(2,1)} %bitcast.186), kind=kOutput, calls=%fused_computation.8 | convolution fusion | flops 545258496 | bytes 19009536 | tf_op jit(solution)/shard_map/qhd,khd->qhk/dot_general | solution.py:96
  158.8 8.6 %fusion.2 = f32[256,4]{0,1:T(4,128)S(1)} fusion(f32[4,256,4096]{2,1,0:T(8,128)} %get-tuple-element.35, f32[256,4]{0,1:T(4,128)S(1)} %broadcast_maximum_fusion), kind=kLoop, calls=%fused_computation.11 | loop fusion | flops 12581888 | bytes 16785408 | tf_op jit(solution)/shard_map/reduce_sum | solution.py:101
  167.5 10.2 %fusion.60 = f32[1,256,4,64]{1,3,2,0:T(8,128)} fusion(bf16[4096,4,64]{0,2,1:T(8,128)(2,1)} %bitcast.188, f32[4,256,4096]{2,1,0:T(8,128)} %get-tuple-element.35, f32[256,4]{0,1:T(4,128)S(1)} %broadcast_maximum_fusion, f32[256,4]{0,1:T(4,128)S(1)} %fusion.2), kind=kOutput, calls=%fused_computation.76 | convolution fusion | flops 549519360 | bytes 19144704 | tf_op jit(solution)/shard_map/qhk,khd->qhd/dot_general | solution.py:102
  177.7 1.2 fusion.63
  179.1 1.9 fusion.139
  181.7 63.8 %all-reduce.5.cloned.1.call-done = f32[256,2304]{1,0:T(8,128)} async-done(((f32[256,2304]{1,0:T(8,128)}), f32[256,2304]{1,0:T(8,128)}) %all-reduce.5.cloned.1.call-update) | async-done | bytes 2359312 | tf_op jit(solution)/shard_map/psum | solution.py:185
  245.5 2.1 multiply_reduce_fusion
  247.7 1.4 copy-done.5
  249.1 1.2 convolution_convert_fusion.2
  250.6 64.6 %all-gather.5.cloned.1.call-done = bf16[1536,2304]{1,0:T(8,128)(2,1)} async-done(((bf16[96,2304]{1,0:T(8,128)(2,1)}), bf16[1536,2304]{1,0:T(8,128)(2,1)}) %all-gather.5.cloned.1.call-update) | async-done | bytes 7077904 | tf_op jit(solution)/shard_map/all_gather | solution.py:208
  315.2 7.7 %fusion.36 = f32[1536,360]{0,1:T(8,128)} fusion(bf16[1536,2304]{1,0:T(8,128)(2,1)} %all-gather.5.cloned.1.call-done, bf16[1,2304,360]{1,2,0:T(8,128)(2,1)} %param.37), kind=kOutput, calls=%fused_computation.57 | convolution fusion | flops 2548039680 | bytes 10948608 | tf_op jit(solution)/shard_map/dot_general | solution.py:209
  322.8 14.3 %fusion.33 = f32[1536,2304]{1,0:T(8,128)} fusion(bf16[1,360,2304]{2,1,0:T(8,128)(2,1)S(1)} %copy-done, bf16[1536,2304]{1,0:T(8,128)(2,1)} %all-gather.5.cloned.1.call-done, f32[1536,360]{0,1:T(8,128)} %fusion.36, bf16[1,2304,360]{1,2,0:T(8,128)(2,1)} %param.38), kind=kOutput, calls=%fused_computation.54 | convolution fusion | flops 5099397120 | bytes 26763264 | tf_op jit(solution)/shard_map/dot_general | solution.py:211
  338.0 2.7 fusion.127
  340.7 3.6 gather_fusion.6
  344.7 92.1 %reduce-scatter.3.cloned.1.call-done = f32[96,2304]{1,0:T(8,128)} async-done(((f32[1536,2304]{1,0:T(8,128)}), f32[96,2304]{1,0:T(8,128)}) %reduce-scatter.3.cloned.1.call-update) | async-done | bytes 884752 | tf_op jit(solution)/shard_map/reduce_scatter | solution.py:216
  436.8 3.9 fusion.72
  441.4 32.1 %reduce-scatter.5.cloned.1.call-done = f32[32,2304]{1,0:T(8,128)} async-done(((f32[256,2304]{1,0:T(8,128)}), f32[32,2304]{1,0:T(8,128)}) %reduce-scatter.5.cloned.1.call-update) | async-done | bytes 294928 | tf_op jit(solution)/shard_map/reduce_scatter | solution.py:219
  473.6 1.8 select_convert_fusion
  (159 shorter events, 20.7 us)
Async XLA Ops:
  6.5 316.3 %copy-start = (bf16[1,360,2304]{2,1,0:T(8,128)(2,1)S(1)}, bf16[1,360,2304]{2,1,0:T(8,128)(2,1)}, u32[]{:S(2)}) copy-start(bf16[1,360,2304]{2,1,0:T(8,128)(2,1)} %param.39) | copy-start | bytes 4976644
  6.5 129.7 %all-gather.3.cloned.1.call-start = ((), (), s32[]{:S(2)}) async-start(), calls=%async_computation.6 | async-start | bytes 4456448 | tf_op jit(solution)/shard_map/all_gather | solution.py:91
  9.6 24.9 %all-to-all-start.1 = ((bf16[16,2,32]{2,1,0:T(2,128)(2,1)}), bf16[16,2,32]{2,1,0:T(2,128)(2,1)S(1)}, u32[]{:S(2)}, u32[]{:S(2)}) async-start(bf16[16,2,32]{2,1,0:T(2,128)(2,1)} %broadcast_in_dim.168), calls=%async_computation.1 | async-start | bytes 16384 | tf_op jit(solution)/shard_map/all_to_all | solution.py:153
  19.3 3.6 copy-start.3
  19.3 3.6 copy-start.6
  19.3 3.6 copy-start.38
  19.4 5.5 %copy-start.35 = (f32[256]{0:T(256)}, f32[256]{0:T(256)S(1)}, u32[]{:S(2)}) copy-start(f32[256]{0:T(256)S(1)} %add_rsqrt_fusion.1) | copy-start | bytes 3076
  23.0 3.0 copy-start.2
  26.6 1.1 copy-start.33
  26.6 4.1 copy-start.10
  26.9 4.9 %copy-start.7 = (bf16[2,2,1024,256]{3,2,1,0:T(8,128)(2,1)S(1)}, bf16[2,2,1024,256]{3,2,1,0:T(8,128)(2,1)}, u32[]{:S(2)}) copy-start(bf16[2,2,1024,256]{3,2,1,0:T(8,128)(2,1)} %param.28) | copy-start | bytes 6291460
  29.2 0.8 copy-start.13
  29.2 3.9 copy-start.24
  31.8 1.4 copy-start.32
  34.5 22.1 %all-to-all-start = ((bf16[16,2,32,256]{3,2,1,0:T(8,128)(2,1)}), bf16[16,2,32,256]{3,2,1,0:T(8,128)(2,1)}, u32[]{:S(2)}, u32[]{:S(2)}) async-start(bf16[16,2,32,256]{3,2,1,0:T(8,128)(2,1)} %pad_maximum_fusion.1), calls=%async_computation | async-start | bytes 1048576 | tf_op jit(solution)/shard_map/all_to_all | solution.py:152
  67.0 2.2 copy-start.18
  67.0 2.2 copy-start.16
  67.1 2.2 copy-start.17
  67.1 2.2 copy-start.37
  69.2 2.8 copy-start.20
  78.7 3.2 copy-start.4
  78.7 3.2 copy-start.19
  78.7 3.2 copy-start.21
  78.7 5.5 %copy-start.15 = (bf16[1,1,1024,256]{2,3,1,0:T(8,128)(2,1)S(1)}, bf16[1,1,1024,256]{2,3,1,0:T(8,128)(2,1)}, u32[]{:S(2)}) copy-start(bf16[1,1,1024,256]{2,3,1,0:T(8,128)(2,1)} %copy.270) | copy-start | bytes 1572868
  82.0 0.7 copy-start.22
  88.7 11.4 %copy-start.8 = (f32[16,1,32,256]{3,2,0,1:T(8,128)S(1)}, f32[16,1,32,256]{3,2,0,1:T(8,128)}, u32[]{:S(2)}) copy-start(f32[16,1,32,256]{3,2,0,1:T(8,128)} %stack_reshape.25) | copy-start | bytes 1572868
  93.0 19.1 %copy-start.25 = (f32[8,32,4]{1,2,0:T(4,128)S(1)}, f32[8,32,4]{1,2,0:T(4,128)}, u32[]{:S(2)}) copy-start(f32[8,32,4]{1,2,0:T(4,128)} %copy-done.24) | copy-start | bytes 12292
  93.0 19.1 %copy-start.26 = (f32[8,32,4]{1,2,0:T(4,128)S(1)}, f32[8,32,4]{1,2,0:T(4,128)}, u32[]{:S(2)}) copy-start(f32[8,32,4]{1,2,0:T(4,128)} %fusion.78) | copy-start | bytes 12292
  93.0 20.4 %copy-start.36 = (f32[256]{0:T(256)S(1)}, f32[256]{0:T(256)}, u32[]{:S(2)}) copy-start(f32[256]{0:T(256)} %copy-done.35) | copy-start | bytes 3076
  93.0 14.6 %all-to-all-start.2 = ((f32[16,1,256]{2,1,0:T(1,128)}), f32[16,1,256]{2,1,0:T(1,128)S(1)}, u32[]{:S(2)}, u32[]{:S(2)}) async-start(f32[16,1,256]{2,1,0:T(1,128)} %reshape.482), calls=%async_computation.2 | async-start | bytes 32768 | tf_op jit(solution)/shard_map/all_to_all | solution.py:170
  107.7 4.3 copy-start.27
  107.7 19.4 %all-to-all-start.3 = ((f32[16,2,32,256]{3,2,1,0:T(8,128)}), f32[16,2,32,256]{3,2,1,0:T(8,128)}, u32[]{:S(2)}, u32[]{:S(2)}) async-start(f32[16,2,32,256]{3,2,1,0:T(8,128)} %pad_maximum_fusion), calls=%async_computation.3 | async-start | bytes 2097152 | tf_op jit(solution)/shard_map/all_to_all | solution.py:169
  112.0 5.7 %copy-start.14 = (f32[8,32,4,32]{1,3,2,0:T(8,128)S(1)}, f32[8,32,4,32]{1,3,2,0:T(8,128)}, u32[]{:S(2)}) copy-start(f32[8,32,4,32]{1,3,2,0:T(8,128)} %copy-done.13) | copy-start | bytes 393220
  112.1 133.5 %all-reduce.5.cloned.1.call-start = ((), (), s32[]{:S(2)}) async-start(), calls=%async_computation.7 | async-start | bytes 4718592 | tf_op jit(solution)/shard_map/psum | solution.py:185
  116.0 4.0 copy-start.34
  167.4 10.2 %copy-start.31 = (f32[256,4]{0,1:T(4,128)S(1)}, f32[256,4]{0,1:T(4,128)}, u32[]{:S(2)}) copy-start(f32[256,4]{0,1:T(4,128)} %add.217) | copy-start | bytes 12292
  167.4 10.2 %copy-start.30 = (f32[1,256,4]{1,2,0:T(4,128)S(1)}, f32[1,256,4]{1,2,0:T(4,128)}, u32[]{:S(2)}) copy-start(f32[1,256,4]{1,2,0:T(4,128)} %add.216) | copy-start | bytes 12292
  167.4 10.3 %copy-start.11 = (f32[1,256,4,64]{1,3,2,0:T(8,128)S(1)}, f32[1,256,4,64]{1,3,2,0:T(8,128)}, u32[]{:S(2)}) copy-start(f32[1,256,4,64]{1,3,2,0:T(8,128)} %copy.282) | copy-start | bytes 786436
  167.4 10.3 %copy-start.12 = (f32[1,256,4,64]{1,3,2,0:T(8,128)S(1)}, f32[1,256,4,64]{1,3,2,0:T(8,128)}, u32[]{:S(2)}) copy-start(f32[1,256,4,64]{1,3,2,0:T(8,128)} %copy.281) | copy-start | bytes 786436
  177.6 1.4 copy-start.9
  179.1 2.0 copy-start.29
  181.0 134.1 %all-gather.5.cloned.1.call-start = ((), (), s32[]{:S(2)}) async-start(), calls=%async_computation.8 | async-start | bytes 7520256 | tf_op jit(solution)/shard_map/all_gather | solution.py:208
  181.7 67.4 %copy-start.28 = (f32[2304]{0:T(1024)S(1)}, f32[2304]{0:T(1024)}, u32[]{:S(2)}) copy-start(f32[2304]{0:T(1024)} %param.34) | copy-start | bytes 27652
  247.6 1.5 copy-start.5
  250.3 186.5 %reduce-scatter.3.cloned.1.call-start = ((), (), s32[]{:S(2)}) async-start(), calls=%async_computation.9 | async-start | bytes 15040512 | tf_op jit(solution)/shard_map/reduce_scatter | solution.py:216
  337.1 0.9 copy-start.23
  337.1 136.4 %reduce-scatter.5.cloned.1.call-start = ((), (), s32[]{:S(2)}) async-start(), calls=%async_computation.10 | async-start | bytes 2654208 | tf_op jit(solution)/shard_map/reduce_scatter | solution.py:219
  436.8 38.6 %copy-start.1 = (bf16[1,360,2304]{2,1,0:T(8,128)(2,1)S(1)}, bf16[1,360,2304]{2,1,0:T(8,128)(2,1)}, u32[]{:S(2)}) copy-start(bf16[1,360,2304]{2,1,0:T(8,128)(2,1)} %param.39) | copy-start | bytes 4976644
Sparse Core Ops, SparseCore 0:
  9.6 59.1 all-gather.2
  181.1 64.3 all-reduce.4
  250.4 64.6 all-gather.4
  337.3 99.4 reduce-scatter.2
  440.8 32.7 reduce-scatter.4
where the time goes:
time: 487 us; the launch traced here: 482 us
  waiting for transfers between devices  263 us (54%)
  matrix products  76.3 us (16%)
  local copies, waits for them, and re-layouts  71.5 us (15%)
  other arithmetic  29.4 us (6%)
  starting transfers between devices  27.5 us (6%)
  between operations  14.7 us (3%)
    reduce_scatter x1, waiting for transfers between devices, on_device(): lax.psum_scatter(partial_out, 'dp', scatter_dimension=0, tiled=True)  92.1 us
    all_gather x1, waiting for transfers between devices, on_device(): piece = lax.all_gather(dispatch, 'dp', axis=0, tiled=True)  64.6 us
    psum x1, waiting for transfers between devices, on_device(): attn_all = lax.psum(projected, 'mp')  63.8 us
    reduce_scatter x1, waiting for transfers between devices, on_device(): mixed = lax.psum_scatter(spread, 'mp', scatter_dimension=0, tiled=True)  32.1 us
    dot_general x1, matrix products, on_device(): jnp.dot((jax.nn.silu(gate_part) * up_part).astype(jnp.bfloat16), down_wei...  14.3 us
    unnamed x87, local copies, waits for them, and re-layouts  13.6 us
    dot_general x1, matrix products, on_device(): jnp.einsum('qhk,khd->qhd', weights.astype(jnp.bfloat16), piece_values, pr...  10.2 us
  transfers between devices with their start and end apart: 9, of which 7 were waited for; matrix products, arithmetic and copies ran while one was open for 20% of the time, Pallas kernels for 0%

commit v1 on v0

--- a/solution.py
+++ b/solution.py
@@ -182,7 +182,7 @@
     projected = jnp.dot(attended, w_out, preferred_element_type=jnp.float32)
     rows_here = tok_rows // lax.axis_size("mp")
     first = lax.axis_index("mp") * rows_here
-    attn_all = lax.psum(projected, "mp")
+    attn_all = jnp.sum(lax.all_gather(projected, "mp"), axis=0)
     resid_all = hidden_in.astype(jnp.float32) + attn_all
     ffn_in = rms_scale(resid_all, ffn_gain).astype(jnp.bfloat16)
     resid = lax.dynamic_slice_in_dim(resid_all, first, rows_here, 0)

time: 487 us -> 525 us (1.078)
  waiting for transfers between devices: 263 us -> 291 us
  other arithmetic: 29.4 us -> 38.6 us
    all_gather x0 -> x1, waiting for transfers between devices: none -> 91.1 us  [on_device(): attn_all = jnp.sum(lax.all_gather(projected, 'mp'), axis=0)]
    psum x1 -> x0, waiting for transfers between devices: 63.8 us -> none  [on_device(): attn_all = lax.psum(projected, 'mp')]
    reduce_sum x0 -> x1, other arithmetic: none -> 9.14 us  [on_device(): attn_all = jnp.sum(lax.all_gather(projected, 'mp'), axis=0)]
  transfers between devices with their start and end apart: 9 -> 9, of which waited for: 7 -> 7; matrix products, arithmetic and copies ran while one was open for 20% -> 19% of each run, Pallas kernels for 0% -> 0%
where the time goes in v1:
time: 525 us; the launch traced here: 520 us
  waiting for transfers between devices  291 us (55%)
  matrix products  76.3 us (15%)
  local copies, waits for them, and re-layouts  71.5 us (14%)
  other arithmetic  38.6 us (7%)
  starting transfers between devices  27.5 us (5%)
  between operations  14.7 us (3%)
    reduce_scatter x1, waiting for transfers between devices, on_device(): lax.psum_scatter(partial_out, 'dp', scatter_dimension=0, tiled=True)  92 us
    all_gather x1, waiting for transfers between devices, on_device(): attn_all = jnp.sum(lax.all_gather(projected, 'mp'), axis=0)  91.1 us
    all_gather x1, waiting for transfers between devices, on_device(): piece = lax.all_gather(dispatch, 'dp', axis=0, tiled=True)  65.7 us
    reduce_scatter x1, waiting for transfers between devices, on_device(): mixed = lax.psum_scatter(spread, 'mp', scatter_dimension=0, tiled=True)  32.1 us
    dot_general x1, matrix products, on_device(): jnp.dot((jax.nn.silu(gate_part) * up_part).astype(jnp.bfloat16), down_wei...  14.3 us
    unnamed x87, local copies, waits for them, and re-layouts  13.6 us
  transfers between devices with their start and end apart: 9, of which 7 were waited for; matrix products, arithmetic and copies ran while one was open for 19% of the time, Pallas kernels for 0%

profile of v1, /device:TPU:0, one launch (start us, length us, event | category | flops | bytes accessed | tf_op | source)
XLA Modules:
  0.0 519.6 jit_solution(5543963637737796681)
XLA Ops:
  9.6 8.1 %all-to-all-start.1 = ((bf16[16,2,32]{2,1,0:T(2,128)(2,1)}), bf16[16,2,32]{2,1,0:T(2,128)(2,1)S(1)}, u32[]{:S(2)}, u32[]{:S(2)}) async-start(bf16[16,2,32]{2,1,0:T(2,128)(2,1)} %broadcast_in_dim.168), calls=%async_computation.1 | async-start | bytes 16384 | tf_op jit(solution)/shard_map/all_to_all | solution.py:153
  17.7 1.6 fusion.30
  19.4 2.5 convolution_convert_fusion.5
  23.0 1.8 convolution_convert_fusion.4
  27.9 1.3 fusion.138
  30.8 1.0 fusion.135
  31.8 1.4 fusion.134
  34.5 7.6 %all-to-all-start = ((bf16[16,2,32,256]{3,2,1,0:T(8,128)(2,1)}), bf16[16,2,32,256]{3,2,1,0:T(8,128)(2,1)}, u32[]{:S(2)}, u32[]{:S(2)}) async-start(bf16[16,2,32,256]{3,2,1,0:T(8,128)(2,1)} %pad_maximum_fusion.1), calls=%async_computation | async-start | bytes 1048576 | tf_op jit(solution)/shard_map/all_to_all | solution.py:152
  42.1 1.2 copy.251
  43.3 2.1 copy.270
  45.4 2.0 copy.290
  47.4 2.0 copy.289
  49.5 2.0 copy.288
  51.5 2.0 copy.291
  54.4 1.6 fusion.97
  56.6 1.9 fusion.136
  58.5 2.0 reshape_squeeze.19
  60.5 2.0 reshape_squeeze.21
  62.5 4.5 bitcast_reduce_fusion.1
  67.1 2.2 fusion.16
  69.3 2.7 fusion.64
  72.0 1.7 copy.274
  73.7 2.6 stack_reshape.25
  76.3 2.4 bitcast_reduce_fusion.2
  78.8 2.6 fusion.14
  82.7 1.5 reshape.483
  84.2 4.5 fusion.69
  88.7 1.7 copy.271
  90.4 2.7 stack_reshape.24
  93.0 7.1 %all-to-all-start.2 = ((f32[16,1,256]{2,1,0:T(1,128)}), f32[16,1,256]{2,1,0:T(1,128)S(1)}, u32[]{:S(2)}, u32[]{:S(2)}) async-start(f32[16,1,256]{2,1,0:T(1,128)} %reshape.483), calls=%async_computation.2 | async-start | bytes 32768 | tf_op jit(solution)/shard_map/all_to_all | solution.py:170
  100.1 2.2 pad_maximum_fusion
  102.3 5.3 %all-to-all-done.2 = f32[16,1,256]{2,1,0:T(1,128)S(1)} async-done(((f32[16,1,256]{2,1,0:T(1,128)}), f32[16,1,256]{2,1,0:T(1,128)S(1)}, u32[]{:S(2)}, u32[]{:S(2)}) %all-to-all-start.2) | async-done | bytes 16416 | tf_op jit(solution)/shard_map/all_to_all | solution.py:170
  107.7 4.3 all-to-all-start.3
  113.5 2.5 convolution_convert_fusion.3
  116.0 1.8 reshape.409
  117.8 1.3 fusion.48
  120.5 1.4 reduce.10
  123.5 3.6 all-to-all-done.3
  127.1 2.5 gather_fusion.5
  129.6 1.2 stack_reshape.27
  131.7 2.5 gather_fusion.4
  134.2 1.2 stack_reshape.26
  136.3 4.5 fusion.133
  140.7 4.3 copy.247
  145.0 4.1 copy.269
  149.1 9.7 %bitcast_reduce_fusion = (f32[256,4]{0,1:T(4,128)S(1)}, f32[4,256,4096]{2,1,0:T(8,128)}) fusion(bf16[256,4,64]{0,2,1:T(8,128)(2,1)S(1)} %bitcast.206, bf16[4096,4,64]{0,2,1:T(8,128)(2,1)} %bitcast.188), kind=kOutput, calls=%fused_computation.8 | convolution fusion | flops 545258496 | bytes 19009536 | tf_op jit(solution)/shard_map/qhd,khd->qhk/dot_general | solution.py:96
  158.8 8.6 %fusion.2 = f32[256,4]{0,1:T(4,128)S(1)} fusion(f32[4,256,4096]{2,1,0:T(8,128)} %get-tuple-element.35, f32[256,4]{0,1:T(4,128)S(1)} %broadcast_maximum_fusion), kind=kLoop, calls=%fused_computation.11 | loop fusion | flops 12581888 | bytes 16785408 | tf_op jit(solution)/shard_map/reduce_sum | solution.py:101
  167.5 10.2 %fusion.60 = f32[1,256,4,64]{1,3,2,0:T(8,128)} fusion(bf16[4096,4,64]{0,2,1:T(8,128)(2,1)} %bitcast.190, f32[4,256,4096]{2,1,0:T(8,128)} %get-tuple-element.35, f32[256,4]{0,1:T(4,128)S(1)} %broadcast_maximum_fusion, f32[256,4]{0,1:T(4,128)S(1)} %fusion.2), kind=kOutput, calls=%fused_computation.76 | convolution fusion | flops 549519360 | bytes 19144704 | tf_op jit(solution)/shard_map/qhk,khd->qhd/dot_general | solution.py:102
  177.7 1.2 fusion.63
  179.1 1.9 fusion.139
  181.7 91.1 %all-gather.9.cloned.1.call-done = f32[2048,2304]{1,0:T(8,128)} async-done(((f32[256,2304]{1,0:T(8,128)}), f32[2048,2304]{1,0:T(8,128)}) %all-gather.9.cloned.1.call-update) | async-done | bytes 18874384 | tf_op jit(solution)/shard_map/all_gather | solution.py:185
  272.8 9.1 %reduce_sum.106 = f32[256,2304]{1,0:T(8,128)} reduce(f32[8,256,2304]{2,1,0:T(8,128)} %bitcast.187, f32[]{:T(128)} %constant.99.clone.1), dimensions={0}, to_apply=%region_11.12 | reduce | flops 4128768 | bytes 21233668 | tf_op jit(solution)/shard_map/reduce_sum | solution.py:185
  281.9 2.1 multiply_reduce_fusion
  284.0 1.4 copy-done.5
  285.5 1.2 convolution_convert_fusion.2
  287.0 65.7 %all-gather.7.cloned.1.call-done = bf16[1536,2304]{1,0:T(8,128)(2,1)} async-done(((bf16[96,2304]{1,0:T(8,128)(2,1)}), bf16[1536,2304]{1,0:T(8,128)(2,1)}) %all-gather.7.cloned.1.call-update) | async-done | bytes 7077904 | tf_op jit(solution)/shard_map/all_gather | solution.py:208
  352.6 7.7 %fusion.36 = f32[1536,360]{0,1:T(8,128)} fusion(bf16[1536,2304]{1,0:T(8,128)(2,1)} %all-gather.7.cloned.1.call-done, bf16[1,2304,360]{1,2,0:T(8,128)(2,1)} %param.37), kind=kOutput, calls=%fused_computation.57 | convolution fusion | flops 2548039680 | bytes 10948608 | tf_op jit(solution)/shard_map/dot_general | solution.py:209
  360.3 14.3 %fusion.33 = f32[1536,2304]{1,0:T(8,128)} fusion(bf16[1,360,2304]{2,1,0:T(8,128)(2,1)S(1)} %copy-done, bf16[1536,2304]{1,0:T(8,128)(2,1)} %all-gather.7.cloned.1.call-done, f32[1536,360]{0,1:T(8,128)} %fusion.36, bf16[1,2304,360]{1,2,0:T(8,128)(2,1)} %param.38), kind=kOutput, calls=%fused_computation.54 | convolution fusion | flops 5099397120 | bytes 26763264 | tf_op jit(solution)/shard_map/dot_general | solution.py:211
  375.4 2.7 fusion.127
  378.2 3.6 gather_fusion.6
  382.2 92.0 %reduce-scatter.3.cloned.1.call-done = f32[96,2304]{1,0:T(8,128)} async-done(((f32[1536,2304]{1,0:T(8,128)}), f32[96,2304]{1,0:T(8,128)}) %reduce-scatter.3.cloned.1.call-update) | async-done | bytes 884752 | tf_op jit(solution)/shard_map/reduce_scatter | solution.py:216
  474.2 3.9 fusion.72
  478.9 32.1 %reduce-scatter.5.cloned.1.call-done = f32[32,2304]{1,0:T(8,128)} async-done(((f32[256,2304]{1,0:T(8,128)}), f32[32,2304]{1,0:T(8,128)}) %reduce-scatter.5.cloned.1.call-update) | async-done | bytes 294928 | tf_op jit(solution)/shard_map/reduce_scatter | solution.py:219
  511.0 1.8 select_convert_fusion
  (160 shorter events, 21.6 us)
Async XLA Ops:
  6.5 353.8 %copy-start = (bf16[1,360,2304]{2,1,0:T(8,128)(2,1)S(1)}, bf16[1,360,2304]{2,1,0:T(8,128)(2,1)}, u32[]{:S(2)}) copy-start(bf16[1,360,2304]{2,1,0:T(8,128)(2,1)} %param.39) | copy-start | bytes 4976644
  6.5 129.7 %all-gather.5.cloned.1.call-start = ((), (), s32[]{:S(2)}) async-start(), calls=%async_computation.6 | async-start | bytes 4456448 | tf_op jit(solution)/shard_map/all_gather | solution.py:91
  9.6 24.9 %all-to-all-start.1 = ((bf16[16,2,32]{2,1,0:T(2,128)(2,1)}), bf16[16,2,32]{2,1,0:T(2,128)(2,1)S(1)}, u32[]{:S(2)}, u32[]{:S(2)}) async-start(bf16[16,2,32]{2,1,0:T(2,128)(2,1)} %broadcast_in_dim.168), calls=%async_computation.1 | async-start | bytes 16384 | tf_op jit(solution)/shard_map/all_to_all | solution.py:153
  19.3 3.6 copy-start.3
  19.3 3.6 copy-start.6
  19.3 3.6 copy-start.38
  19.4 5.5 %copy-start.35 = (f32[256]{0:T(256)}, f32[256]{0:T(256)S(1)}, u32[]{:S(2)}) copy-start(f32[256]{0:T(256)S(1)} %add_rsqrt_fusion.1) | copy-start | bytes 3076
  23.0 3.0 copy-start.2
  26.6 1.1 copy-start.33
  26.6 4.1 copy-start.10
  26.9 4.9 copy-start.7
  29.2 0.8 copy-start.13
  29.2 3.9 copy-start.24
  31.8 1.4 copy-start.32
  34.5 22.1 %all-to-all-start = ((bf16[16,2,32,256]{3,2,1,0:T(8,128)(2,1)}), bf16[16,2,32,256]{3,2,1,0:T(8,128)(2,1)}, u32[]{:S(2)}, u32[]{:S(2)}) async-start(bf16[16,2,32,256]{3,2,1,0:T(8,128)(2,1)} %pad_maximum_fusion.1), calls=%async_computation | async-start | bytes 1048576 | tf_op jit(solution)/shard_map/all_to_all | solution.py:152
  67.0 2.2 copy-start.18
  67.0 2.2 copy-start.16
  67.1 2.2 copy-start.17
  67.1 2.2 copy-start.37
  69.2 2.8 copy-start.20
  78.7 3.2 copy-start.4
  78.7 3.2 copy-start.19
  78.7 3.2 copy-start.21
  78.7 5.5 %copy-start.15 = (bf16[1,1,1024,256]{2,3,1,0:T(8,128)(2,1)S(1)}, bf16[1,1,1024,256]{2,3,1,0:T(8,128)(2,1)}, u32[]{:S(2)}) copy-start(bf16[1,1,1024,256]{2,3,1,0:T(8,128)(2,1)} %copy.270) | copy-start | bytes 1572868
  82.0 0.7 copy-start.22
  88.7 11.4 %copy-start.8 = (f32[16,1,32,256]{3,2,0,1:T(8,128)S(1)}, f32[16,1,32,256]{3,2,0,1:T(8,128)}, u32[]{:S(2)}) copy-start(f32[16,1,32,256]{3,2,0,1:T(8,128)} %stack_reshape.25) | copy-start | bytes 1572868
  93.0 19.1 %copy-start.25 = (f32[8,32,4]{1,2,0:T(4,128)S(1)}, f32[8,32,4]{1,2,0:T(4,128)}, u32[]{:S(2)}) copy-start(f32[8,32,4]{1,2,0:T(4,128)} %copy-done.24) | copy-start | bytes 12292
  93.0 19.1 %copy-start.26 = (f32[8,32,4]{1,2,0:T(4,128)S(1)}, f32[8,32,4]{1,2,0:T(4,128)}, u32[]{:S(2)}) copy-start(f32[8,32,4]{1,2,0:T(4,128)} %fusion.78) | copy-start | bytes 12292
  93.0 20.4 %copy-start.36 = (f32[256]{0:T(256)S(1)}, f32[256]{0:T(256)}, u32[]{:S(2)}) copy-start(f32[256]{0:T(256)} %copy-done.35) | copy-start | bytes 3076
  93.0 14.6 %all-to-all-start.2 = ((f32[16,1,256]{2,1,0:T(1,128)}), f32[16,1,256]{2,1,0:T(1,128)S(1)}, u32[]{:S(2)}, u32[]{:S(2)}) async-start(f32[16,1,256]{2,1,0:T(1,128)} %reshape.483), calls=%async_computation.2 | async-start | bytes 32768 | tf_op jit(solution)/shard_map/all_to_all | solution.py:170
  107.7 4.3 copy-start.27
  107.7 19.4 %all-to-all-start.3 = ((f32[16,2,32,256]{3,2,1,0:T(8,128)}), f32[16,2,32,256]{3,2,1,0:T(8,128)}, u32[]{:S(2)}, u32[]{:S(2)}) async-start(f32[16,2,32,256]{3,2,1,0:T(8,128)} %pad_maximum_fusion), calls=%async_computation.3 | async-start | bytes 2097152 | tf_op jit(solution)/shard_map/all_to_all | solution.py:169
  112.0 5.7 %copy-start.14 = (f32[8,32,4,32]{1,3,2,0:T(8,128)S(1)}, f32[8,32,4,32]{1,3,2,0:T(8,128)}, u32[]{:S(2)}) copy-start(f32[8,32,4,32]{1,3,2,0:T(8,128)} %copy-done.13) | copy-start | bytes 393220
  112.1 160.7 %all-gather.9.cloned.1.call-start = ((), (), s32[]{:S(2)}) async-start(), calls=%async_computation.10 | async-start | bytes 21233664 | tf_op jit(solution)/shard_map/all_gather | solution.py:185
  116.0 4.0 copy-start.34
  167.4 10.2 %copy-start.31 = (f32[256,4]{0,1:T(4,128)S(1)}, f32[256,4]{0,1:T(4,128)}, u32[]{:S(2)}) copy-start(f32[256,4]{0,1:T(4,128)} %add.215) | copy-start | bytes 12292
  167.4 10.2 %copy-start.30 = (f32[1,256,4]{1,2,0:T(4,128)S(1)}, f32[1,256,4]{1,2,0:T(4,128)}, u32[]{:S(2)}) copy-start(f32[1,256,4]{1,2,0:T(4,128)} %add.214) | copy-start | bytes 12292
  167.4 10.3 %copy-start.11 = (f32[1,256,4,64]{1,3,2,0:T(8,128)S(1)}, f32[1,256,4,64]{1,3,2,0:T(8,128)}, u32[]{:S(2)}) copy-start(f32[1,256,4,64]{1,3,2,0:T(8,128)} %copy.282) | copy-start | bytes 786436
  167.4 10.3 %copy-start.12 = (f32[1,256,4,64]{1,3,2,0:T(8,128)S(1)}, f32[1,256,4,64]{1,3,2,0:T(8,128)}, u32[]{:S(2)}) copy-start(f32[1,256,4,64]{1,3,2,0:T(8,128)} %copy.281) | copy-start | bytes 786436
  177.6 1.4 copy-start.9
  179.1 2.0 copy-start.29
  181.0 171.6 %all-gather.7.cloned.1.call-start = ((), (), s32[]{:S(2)}) async-start(), calls=%async_computation.7 | async-start | bytes 7520256 | tf_op jit(solution)/shard_map/all_gather | solution.py:208
  281.9 3.6 copy-start.28
  284.0 1.5 copy-start.5
  286.7 187.5 %reduce-scatter.3.cloned.1.call-start = ((), (), s32[]{:S(2)}) async-start(), calls=%async_computation.8 | async-start | bytes 15040512 | tf_op jit(solution)/shard_map/reduce_scatter | solution.py:216
  374.6 0.9 copy-start.23
  374.6 136.4 %reduce-scatter.5.cloned.1.call-start = ((), (), s32[]{:S(2)}) async-start(), calls=%async_computation.9 | async-start | bytes 2654208 | tf_op jit(solution)/shard_map/reduce_scatter | solution.py:219
  474.2 38.6 %copy-start.1 = (bf16[1,360,2304]{2,1,0:T(8,128)(2,1)S(1)}, bf16[1,360,2304]{2,1,0:T(8,128)(2,1)}, u32[]{:S(2)}) copy-start(bf16[1,360,2304]{2,1,0:T(8,128)(2,1)} %param.39) | copy-start | bytes 4976644
Sparse Core Ops, SparseCore 0:
  9.6 59.1 all-gather.4
  181.1 91.6 all-gather.8
  286.8 65.7 all-gather.6
  374.7 99.4 reduce-scatter.2
  478.2 32.7 reduce-scatter.4
